TPU v7x, 32 devices: a whole 2x2x4 slice. The times are simulated.
32 devices in a mesh: patch: 8 (over z, x), lat: 4 (over y, core).
Axes of the slice: x: 2, y: 2, z: 4, core: 2. Of those that a mesh axis runs over, the one named last changes fastest.
Arguments:
- obs_values: bfloat16 [4096, 96], P(('patch', 'lat')), may hold values from -6 to 6
- obs_count: int32 [32, 32], P(('patch', 'lat')), may hold values from 0 to 4, as said below
- obs_node: int32 [4096, 3], P(('patch', 'lat')), may hold values from 0 to 319
- mesh_init: bfloat16 [10240, 512], P(('patch', 'lat')), may hold values from -6 to 6
- mesh_offset: int32 [10240, 6], P(('patch', 'lat')), may hold values from -128 to 128, as said below
- weights_flat: bfloat16 [32, 75264], P(('patch', 'lat')), may hold values from -0.25 to 0.25
- edge_bias: float32 [2, 512], replicated, may hold values from -3 to 3
- node_bias: float32 [2, 512], replicated, may hold values from -3 to 3
- norm_gain: float32 [2, 512], replicated, may hold values from 0.1 to 1.9
Outputs:
- mesh_latent: bfloat16 [10240, 512], P(('patch', 'lat'))
Inputs may be any that keep to these rules, and one draw needn't show every extreme that they name: obs_count[s, d] counts the live slots (the first ones) among the 4 slots that device s holds for device d; each source fills all 4 slots for some destination, and some destination receives 4 live slots from every source. `obs_node`: local node on the destination device. The k-th incoming edge of node n comes from node (n + mesh_offset[n, k]) mod 10240; offsets of both -128 and 128 occur.
All inputs are finite; a program needn't handle non-finite values.
Results may differ from a plain program's by a relative error of at most 0.0085.
Values may be sent and summed in bfloat16 or wider, within the bound.
No kernel may reach another device: no remote copies, remote signals or barrier semaphores. Data moves between devices by JAX's collectives and lax.ppermute only.
A program may use at most 128 MiB of HBM per device.

v0:
```python
import jax
import jax.numpy as jnp
from jax import lax
from jax.sharding import PartitionSpec as P

D = 512
CH = 96
OBS_EDGES = 3
DEG = 6
HALO = 128


def extended(block, sides, width):
    for axis, dim in sides:
        count = lax.axis_size(axis)
        forward = [(i, i + 1) for i in range(count - 1)]
        forward.append((count - 1, 0))
        backward = [(target, source) for source, target in forward]
        low = lax.ppermute(
            lax.slice_in_dim(block, block.shape[dim] - width, None, axis=dim), axis, forward
        )
        high = lax.ppermute(lax.slice_in_dim(block, 0, width, axis=dim), axis, backward)
        block = jnp.concatenate([low, block, high], axis=dim)
    return block


def unpack(flat):
    shapes = ((CH, D), (D, 2 * D), (D, D), (D, D), (D, 3 * D), (D, D), (D, D))
    pieces = []
    offset = 0
    for height, breadth in shapes:
        pieces.append(flat[offset : offset + height * breadth].reshape(height, breadth))
        offset = offset + height * breadth
    return pieces


def layer_norm(values, gain):
    center = values - jnp.mean(values, axis=-1, keepdims=True)
    spread = jnp.mean(center * center, axis=-1, keepdims=True)
    return center * lax.rsqrt(spread + 1e-05) * gain


def embed_rows(rows, w_in):
    return jnp.dot(rows, w_in, preferred_element_type=jnp.float32).astype(jnp.bfloat16)


def deliver(values, nodes, counts):
    return (
        lax.all_to_all(
            lax.all_to_all(values, "patch", split_axis=0, concat_axis=0, tiled=True),
            "lat",
            split_axis=1,
            concat_axis=1,
            tiled=True,
        ),
        lax.all_to_all(
            lax.all_to_all(nodes, "patch", split_axis=0, concat_axis=0, tiled=True),
            "lat",
            split_axis=1,
            concat_axis=1,
            tiled=True,
        ),
        lax.all_to_all(
            lax.all_to_all(counts, "patch", split_axis=0, concat_axis=0, tiled=True),
            "lat",
            split_axis=1,
            concat_axis=1,
            tiled=True,
        ),
    )


def shards(
    obs_values,
    obs_count,
    obs_node,
    mesh_init,
    mesh_offset,
    weights_flat,
    edge_bias,
    node_bias,
    norm_gain,
):
    n_patch = lax.axis_size("patch")
    n_lat = lax.axis_size("lat")
    senders = n_patch * n_lat
    capacity = obs_values.shape[0] // senders
    node_dev = mesh_init.shape[0]
    table = lax.all_gather(weights_flat, ("patch", "lat"), axis=0, tiled=True)
    w_in, w_enc, w_agg, w_out, w_proc, w_pagg, w_pout = unpack(table.reshape(-1))
    breadth = obs_values.shape[1]
    arrived, targets, counts = deliver(
        obs_values.reshape(n_patch, n_lat, capacity, breadth),
        obs_node.reshape(n_patch, n_lat, capacity, OBS_EDGES),
        obs_count.reshape(n_patch, n_lat),
    )
    arrived = arrived.reshape(senders * capacity, breadth)
    targets = targets.reshape(senders * capacity, OBS_EDGES)
    embedded = embed_rows(arrived, w_in)
    alive = (
        (jnp.arange(capacity, dtype=jnp.int32)[None, :] < counts.reshape(senders, 1))
        .astype(jnp.float32)
        .reshape(-1)
    )
    encoded = jnp.dot(mesh_init, w_enc, preferred_element_type=jnp.float32)
    query = encoded[:, :D] + edge_bias[0]
    total_rows = senders * capacity
    block = min(512, total_rows)
    turns = total_rows // block
    node_ids = jnp.arange(node_dev, dtype=jnp.int32)[None, :]

    def encode_block(block_index, totals):
        start = block_index * block
        piece = lax.dynamic_slice_in_dim(embedded, start, block, 0).astype(jnp.float32)
        nodes = lax.dynamic_slice_in_dim(targets, start, block, 0)
        weight = lax.dynamic_slice_in_dim(alive, start, block, 0)[:, None]
        for which in range(OBS_EDGES):
            selector = (nodes[:, which][:, None] == node_ids).astype(jnp.float32)
            picked = jnp.dot(selector, query, precision=lax.Precision.HIGHEST)
            message = jax.nn.silu(piece + picked) * weight
            totals = totals + lax.dot_general(
                selector, message, (((0,), (0,)), ((), ())), precision=lax.Precision.HIGHEST
            )
        return totals

    totals = lax.fori_loop(0, turns, encode_block, jnp.zeros((node_dev, D), jnp.float32))
    gathered = totals.astype(jnp.bfloat16)
    hidden = jax.nn.silu(
        encoded[:, D:] + jnp.dot(gathered, w_agg, preferred_element_type=jnp.float32) + node_bias[0]
    ).astype(jnp.bfloat16)
    first = (
        mesh_init.astype(jnp.float32)
        + layer_norm(jnp.dot(hidden, w_out, preferred_element_type=jnp.float32), norm_gain[0])
    ).astype(jnp.bfloat16)
    projected = jnp.dot(first, w_proc, preferred_element_type=jnp.float32)
    sources = projected[:, :D].astype(jnp.bfloat16)
    target = projected[:, D : 2 * D] + edge_bias[1]
    padded = extended(sources, ((("patch", "lat"), 0),), HALO)
    local_ids = jnp.arange(node_dev, dtype=jnp.int32) + HALO
    pooled = jnp.zeros((node_dev, D), jnp.float32)
    for which in range(DEG):
        anchor = local_ids + mesh_offset[:, which]
        pooled = pooled + jax.nn.silu(jnp.take(padded, anchor, axis=0).astype(jnp.float32) + target)
    hidden2 = jax.nn.silu(
        projected[:, 2 * D :]
        + jnp.dot(pooled.astype(jnp.bfloat16), w_pagg, preferred_element_type=jnp.float32)
        + node_bias[1]
    ).astype(jnp.bfloat16)
    return (
        first.astype(jnp.float32)
        + layer_norm(jnp.dot(hidden2, w_pout, preferred_element_type=jnp.float32), norm_gain[1])
    ).astype(jnp.bfloat16)


def solution(mesh):
    return jax.shard_map(
        shards,
        mesh=mesh,
        in_specs=(
            P(("patch", "lat"), None),
            P(("patch", "lat"), None),
            P(("patch", "lat"), None),
            P(("patch", "lat"), None),
            P(("patch", "lat"), None),
            P(("patch", "lat"), None),
            P(),
            P(),
            P(),
        ),
        out_specs=P(("patch", "lat"), None),
        check_vma=False,
    )
```

profile of v0, /device:TPU:0, one launch (start us, length us, event | category | flops | bytes accessed | tf_op | source)
XLA Modules:
  0.0 260.3 jit_solution(6021291949161695831)
XLA Ops:
  9.8 7.3 %all-to-all-start.4 = ((s32[8,1,4]{2,1,0:T(1,128)}), s32[8,1,4]{2,1,0:T(1,128)S(1)}, u32[]{:S(2)}, u32[]{:S(2)}) async-start(s32[8,1,4]{2,1,0:T(1,128)} %bitcast.5), calls=%async_computation.4 | async-start | bytes 8192 | tf_op jit(solution)/shard_map/all_to_all | solution.py:64
  23.5 5.9 %all-to-all-start = ((s32[8,4,4,3]{2,1,3,0:T(4,128)}), s32[8,4,4,3]{2,1,3,0:T(4,128)S(1)}, u32[]{:S(2)}, u32[]{:S(2)}) async-start(s32[8,4,4,3]{2,1,3,0:T(4,128)} %copy.15), calls=%async_computation | async-start | bytes 98304 | tf_op jit(solution)/shard_map/all_to_all | solution.py:57
  30.1 6.2 %all-to-all-done = s32[8,4,4,3]{2,1,3,0:T(4,128)S(1)} async-done(((s32[8,4,4,3]{2,1,3,0:T(4,128)}), s32[8,4,4,3]{2,1,3,0:T(4,128)S(1)}, u32[]{:S(2)}, u32[]{:S(2)}) %all-to-all-start) | async-done | bytes 1568 | tf_op jit(solution)/shard_map/all_to_all | solution.py:57
  36.3 3.2 %all-to-all-start.5 = ((s32[8,4,1]{0,2,1:T(1,128)}), s32[8,4,1]{0,2,1:T(1,128)S(1)}, u32[]{:S(2)}, u32[]{:S(2)}) async-start(s32[8,4,1]{0,2,1:T(1,128)} %copy.23), calls=%async_computation.5 | async-start | bytes 4096 | tf_op jit(solution)/shard_map/all_to_all | solution.py:63
  40.3 3.0 %all-to-all-done.5 = s32[8,4,1]{0,2,1:T(1,128)S(1)} async-done(((s32[8,4,1]{0,2,1:T(1,128)}), s32[8,4,1]{0,2,1:T(1,128)S(1)}, u32[]{:S(2)}, u32[]{:S(2)}) %all-to-all-start.5) | async-done | bytes 160 | tf_op jit(solution)/shard_map/all_to_all | solution.py:63
  43.3 3.3 %all-to-all-start.1 = ((s32[8,4,4,3]{0,2,3,1:T(4,128)}), s32[8,4,4,3]{0,2,3,1:T(4,128)S(1)}, u32[]{:S(2)}, u32[]{:S(2)}) async-start(s32[8,4,4,3]{0,2,3,1:T(4,128)} %copy.16), calls=%async_computation.1 | async-start | bytes 49152 | tf_op jit(solution)/shard_map/all_to_all | solution.py:56
  48.2 2.2 all-to-all-done.1
  50.4 3.3 %all-to-all-start.2 = ((bf16[8,4,4,96]{3,2,1,0:T(4,128)(2,1)}), bf16[8,4,4,96]{3,2,1,0:T(4,128)(2,1)S(1)}, u32[]{:S(2)}, u32[]{:S(2)}) async-start(bf16[8,4,4,96]{3,2,1,0:T(4,128)(2,1)} %bitcast.2), calls=%async_computation.2 | async-start | bytes 65536 | tf_op jit(solution)/shard_map/all_to_all | solution.py:50
  54.2 6.2 %all-to-all-done.2 = bf16[8,4,4,96]{3,2,1,0:T(4,128)(2,1)S(1)} async-done(((bf16[8,4,4,96]{3,2,1,0:T(4,128)(2,1)}), bf16[8,4,4,96]{3,2,1,0:T(4,128)(2,1)S(1)}, u32[]{:S(2)}, u32[]{:S(2)}) %all-to-all-start.2) | async-done | bytes 24608 | tf_op jit(solution)/shard_map/all_to_all | solution.py:50
  61.0 3.3 %all-to-all-start.3 = ((bf16[8,4,4,96]{3,2,0,1:T(4,128)(2,1)}), bf16[8,4,4,96]{3,2,0,1:T(4,128)(2,1)S(1)}, u32[]{:S(2)}, u32[]{:S(2)}) async-start(bf16[8,4,4,96]{3,2,0,1:T(4,128)(2,1)} %copy.19), calls=%async_computation.3 | async-start | bytes 65536 | tf_op jit(solution)/shard_map/all_to_all | solution.py:49
  64.3 4.3 %all-to-all-done.3 = bf16[8,4,4,96]{3,2,0,1:T(4,128)(2,1)S(1)} async-done(((bf16[8,4,4,96]{3,2,0,1:T(4,128)(2,1)}), bf16[8,4,4,96]{3,2,0,1:T(4,128)(2,1)S(1)}, u32[]{:S(2)}, u32[]{:S(2)}) %all-to-all-start.3) | async-done | bytes 24608 | tf_op jit(solution)/shard_map/all_to_all | solution.py:49
  68.6 27.7 %all-gather.3.cloned.1.call-done = bf16[32,1,75264]{2,1,0:T(2,128)(2,1)} async-done(((bf16[1,1,75264]{2,1,0:T(2,128)(2,1)}), bf16[32,1,75264]{2,1,0:T(2,128)(2,1)}) %all-gather.3.cloned.1.call-update) | async-done | bytes 4816912 | tf_op jit(solution)/shard_map/all_gather | solution.py:89
  96.3 87.6 %reduce = bf16[32,75264]{1,0:T(8,128)(2,1)} reduce(bf16[32,1,75264]{2,1,0:T(2,128)(2,1)} %all-gather.3.cloned.1.call-done, bf16[]{:T(256)} %constant.49), dimensions={1}, to_apply=%all-gather.reduce_sub_computation | reduce | bytes 9633794 | tf_op jit(solution)/shard_map/all_gather | solution.py:89
  183.9 9.6 %slice.107 = bf16[4704,512]{1,0:T(8,128)(2,1)} reshape(bf16[32,75264]{1,0:T(8,128)(2,1)} %reduce) | data formatting | bytes 9633792 | tf_op jit(solution)/shard_map/slice | solution.py:32
  193.5 10.3 %slice.103 = bf16[2352,1024]{1,0:T(8,128)(2,1)} reshape(bf16[32,75264]{1,0:T(8,128)(2,1)} %reduce) | data formatting | bytes 9633792 | tf_op jit(solution)/shard_map/slice | solution.py:32
  203.8 9.7 %reshape.98 = bf16[2408448]{0:T(1024)(128)(2,1)} reshape(bf16[32,75264]{1,0:T(8,128)(2,1)} %reduce) | data formatting | bytes 9633792 | tf_op jit(solution)/shard_map/reshape | solution.py:90
  228.5 5.1 %collective-permute-start.1 = (bf16[128,512]{1,0:T(8,128)(2,1)S(1)}, bf16[128,512]{1,0:T(8,128)(2,1)S(1)}, u32[]{:S(2)}, u32[]{:S(2)}) collective-permute-start(bf16[128,512]{1,0:T(8,128)(2,1)S(1)} %get-tuple-element.37), channel_id=1, source_target_pairs={{1,0},{2,1},{3,2},{4,3},{5,4},{6,5},{7,6},{8,7},{9,8},{10,9},{11,1... | collective-permute-start | bytes 393224 | tf_op jit(solution)/shard_map/ppermute | solution.py:22
  233.7 2.6 collective-permute-done
  236.3 2.2 gather_fusion.4
  238.6 2.0 gather_fusion
  240.6 2.0 gather_fusion.1
  242.6 2.0 gather_fusion.2
  244.7 2.0 gather_fusion.3
  248.7 3.5 %fusion.84 = (f32[320]{0:T(512)S(1)}, f32[320,512]{1,0:T(8,128)S(1)}) fusion(bf16[4704,512]{1,0:T(8,128)(2,1)} %slice.107, f32[320,1536]{1,0:T(8,128)} %get-tuple-element.50, f32[512]{0:T(512)S(1)} %bitcast.37, bf16[320,512]{1,0:T(8,128)(2,1)S(1)} %gather_fusion.5, bf16[320,512]{1,0:T(8,128)(2,1)S(1)} %gather_fusion.4, ...), kind=kOutput, calls=%fused_computation.131 | convolution fusion | flops 344882880 | bytes 4988992 | tf_op jit(solution)/shard_map/dot_general | solution.py:151
  (67 shorter events, 31.9 us)
Async XLA Ops:
  6.5 89.8 %all-gather.3.cloned.1.call-start = ((), (), s32[]{:S(2)}) async-start(), calls=%async_computation.6 | async-start | bytes 9934848 | tf_op jit(solution)/shard_map/all_gather | solution.py:89
  9.8 13.8 %all-to-all-start.4 = ((s32[8,1,4]{2,1,0:T(1,128)}), s32[8,1,4]{2,1,0:T(1,128)S(1)}, u32[]{:S(2)}, u32[]{:S(2)}) async-start(s32[8,1,4]{2,1,0:T(1,128)} %bitcast.5), calls=%async_computation.4 | async-start | bytes 8192 | tf_op jit(solution)/shard_map/all_to_all | solution.py:64
  23.5 12.8 %all-to-all-start = ((s32[8,4,4,3]{2,1,3,0:T(4,128)}), s32[8,4,4,3]{2,1,3,0:T(4,128)S(1)}, u32[]{:S(2)}, u32[]{:S(2)}) async-start(s32[8,4,4,3]{2,1,3,0:T(4,128)} %copy.15), calls=%async_computation | async-start | bytes 98304 | tf_op jit(solution)/shard_map/all_to_all | solution.py:57
  36.3 7.0 %all-to-all-start.5 = ((s32[8,4,1]{0,2,1:T(1,128)}), s32[8,4,1]{0,2,1:T(1,128)S(1)}, u32[]{:S(2)}, u32[]{:S(2)}) async-start(s32[8,4,1]{0,2,1:T(1,128)} %copy.23), calls=%async_computation.5 | async-start | bytes 4096 | tf_op jit(solution)/shard_map/all_to_all | solution.py:63
  43.3 7.1 %all-to-all-start.1 = ((s32[8,4,4,3]{0,2,3,1:T(4,128)}), s32[8,4,4,3]{0,2,3,1:T(4,128)S(1)}, u32[]{:S(2)}, u32[]{:S(2)}) async-start(s32[8,4,4,3]{0,2,3,1:T(4,128)} %copy.16), calls=%async_computation.1 | async-start | bytes 49152 | tf_op jit(solution)/shard_map/all_to_all | solution.py:56
  50.4 10.0 %all-to-all-start.2 = ((bf16[8,4,4,96]{3,2,1,0:T(4,128)(2,1)}), bf16[8,4,4,96]{3,2,1,0:T(4,128)(2,1)S(1)}, u32[]{:S(2)}, u32[]{:S(2)}) async-start(bf16[8,4,4,96]{3,2,1,0:T(4,128)(2,1)} %bitcast.2), calls=%async_computation.2 | async-start | bytes 65536 | tf_op jit(solution)/shard_map/all_to_all | solution.py:50
  61.0 7.6 %all-to-all-start.3 = ((bf16[8,4,4,96]{3,2,0,1:T(4,128)(2,1)}), bf16[8,4,4,96]{3,2,0,1:T(4,128)(2,1)S(1)}, u32[]{:S(2)}, u32[]{:S(2)}) async-start(bf16[8,4,4,96]{3,2,0,1:T(4,128)(2,1)} %copy.19), calls=%async_computation.3 | async-start | bytes 65536 | tf_op jit(solution)/shard_map/all_to_all | solution.py:49
  203.8 10.8 %copy-start.1 = (bf16[320,512]{1,0:T(8,128)(2,1)S(1)}, bf16[320,512]{1,0:T(8,128)(2,1)}, u32[]{:S(2)}) copy-start(bf16[320,512]{1,0:T(8,128)(2,1)} %param.14) | copy-start | bytes 983044
  221.5 0.8 copy-start
  221.5 1.6 slice-start
  228.2 8.0 %collective-permute-start = (bf16[128,512]{1,0:T(8,128)(2,1)S(1)}, bf16[128,512]{1,0:T(8,128)(2,1)S(1)}, u32[]{:S(2)}, u32[]{:S(2)}) collective-permute-start(bf16[128,512]{1,0:T(8,128)(2,1)S(1)} %get-tuple-element.36), channel_id=1, source_target_pairs={{0,1},{1,2},{2,3},{3,4},{4,5},{5,6},{6,7},{7,8},{8,9},{9,10},{10,1... | collective-permute-start | bytes 393224 | tf_op jit(solution)/shard_map/ppermute | solution.py:19
  228.5 7.7 %collective-permute-start.1 = (bf16[128,512]{1,0:T(8,128)(2,1)S(1)}, bf16[128,512]{1,0:T(8,128)(2,1)S(1)}, u32[]{:S(2)}, u32[]{:S(2)}) collective-permute-start(bf16[128,512]{1,0:T(8,128)(2,1)S(1)} %get-tuple-element.37), channel_id=1, source_target_pairs={{1,0},{2,1},{3,2},{4,3},{5,4},{6,5},{7,6},{8,7},{9,8},{10,9},{11,1... | collective-permute-start | bytes 393224 | tf_op jit(solution)/shard_map/ppermute | solution.py:22
Sparse Core Ops, SparseCore 0:
  10.2 86.1 all-gather.2
where the time goes:
time: 261 us; the launch traced here: 260 us
  other arithmetic  93.5 us (36%)
  local copies, waits for them, and re-layouts  55.1 us (21%)
  waiting for transfers between devices  53 us (20%)
  starting transfers between devices  31.7 us (12%)
  between operations  13.7 us (5%)
  matrix products  13.4 us (5%)
    all_gather x1, other arithmetic, shards(): table = lax.all_gather(weights_flat, ('patch', 'lat'), axis=0, tiled=True)  87.6 us
    all_gather x1, waiting for transfers between devices, shards(): table = lax.all_gather(weights_flat, ('patch', 'lat'), axis=0, tiled=True)  27.7 us
    slice x4, local copies, waits for them, and re-layouts, unpack(): flat[offset:offset + height * breadth].reshape(height, breadth)  20.7 us
    gather x6, local copies, waits for them, and re-layouts, shards(): jnp.take(padded, anchor, axis=0).astype(jnp.float32) + target  12.4 us
    reshape x1, local copies, waits for them, and re-layouts, shards(): table.reshape(-1)  9.71 us
    all_to_all x1, starting transfers between devices, deliver(): lax.all_to_all(counts, 'patch', split_axis=0, concat_axis=0, tiled=True)  7.28 us
    all_to_all x1, waiting for transfers between devices, deliver(): lax.all_to_all(nodes, 'patch', split_axis=0, concat_axis=0, tiled=True)  6.21 us
    all_to_all x1, waiting for transfers between devices, deliver(): lax.all_to_all(values, 'patch', split_axis=0, concat_axis=0, tiled=True)  6.17 us
  transfers between devices with their start and end apart: 9, of which 8 were waited for; matrix products, arithmetic and copies ran while one was open for 5% of the time, Pallas kernels for 0%

commit v1 on v0

--- a/solution.py
+++ b/solution.py
@@ -46,12 +46,20 @@
 
 def deliver(values, nodes, counts):
     return (
-        lax.all_to_all(
-            lax.all_to_all(values, "patch", split_axis=0, concat_axis=0, tiled=True),
-            "lat",
-            split_axis=1,
-            concat_axis=1,
-            tiled=True,
+        jnp.concatenate(
+            lax.all_to_all(
+                jnp.stack(
+                    jnp.split(
+                        lax.all_to_all(values, "patch", split_axis=0, concat_axis=0, tiled=True),
+                        lax.axis_size("lat"),
+                        axis=1,
+                    )
+                ),
+                "lat",
+                0,
+                0,
+            ),
+            axis=1,
         ),
         lax.all_to_all(
             lax.all_to_all(nodes, "patch", split_axis=0, concat_axis=0, tiled=True),

time: 261 us -> 261 us (level)
  no operation moved by 1% of the time
where the time goes in v1:
time: 261 us; the launch traced here: 260 us
  other arithmetic  94.1 us (36%)
  local copies, waits for them, and re-layouts  54.5 us (21%)
  waiting for transfers between devices  53 us (20%)
  starting transfers between devices  31.7 us (12%)
  between operations  13.7 us (5%)
  matrix products  13.4 us (5%)
    all_gather x1, other arithmetic, shards(): table = lax.all_gather(weights_flat, ('patch', 'lat'), axis=0, tiled=True)  87.6 us
    all_gather x1, waiting for transfers between devices, shards(): table = lax.all_gather(weights_flat, ('patch', 'lat'), axis=0, tiled=True)  27.9 us
    slice x4, local copies, waits for them, and re-layouts, unpack(): flat[offset:offset + height * breadth].reshape(height, breadth)  20.7 us
    gather x6, local copies, waits for them, and re-layouts, shards(): jnp.take(padded, anchor, axis=0).astype(jnp.float32) + target  12.4 us
    reshape x1, local copies, waits for them, and re-layouts, shards(): table.reshape(-1)  9.73 us
    all_to_all x1, starting transfers between devices, deliver(): lax.all_to_all(counts, 'patch', split_axis=0, concat_axis=0, tiled=True)  7.28 us
    all_to_all x1, waiting for transfers between devices, deliver(): lax.all_to_all(nodes, 'patch', split_axis=0, concat_axis=0, tiled=True)  6.17 us
    all_to_all x1, waiting for transfers between devices, deliver(): lax.all_to_all(values, 'patch', split_axis=0, concat_axis=0, tiled=True)  6.17 us
  transfers between devices with their start and end apart: 9, of which 8 were waited for; matrix products, arithmetic and copies ran while one was open for 5% of the time, Pallas kernels for 0%

profile of v1, /device:TPU:0, one launch (start us, length us, event | category | flops | bytes accessed | tf_op | source)
XLA Modules:
  0.0 260.4 jit_solution(8363554263484191776)
XLA Ops:
  9.8 7.3 %all-to-all-start.4 = ((s32[8,1,4]{2,1,0:T(1,128)}), s32[8,1,4]{2,1,0:T(1,128)S(1)}, u32[]{:S(2)}, u32[]{:S(2)}) async-start(s32[8,1,4]{2,1,0:T(1,128)} %bitcast.10), calls=%async_computation.4 | async-start | bytes 8192 | tf_op jit(solution)/shard_map/all_to_all | solution.py:72
  23.5 5.9 %all-to-all-start = ((s32[8,4,4,3]{2,1,3,0:T(4,128)}), s32[8,4,4,3]{2,1,3,0:T(4,128)S(1)}, u32[]{:S(2)}, u32[]{:S(2)}) async-start(s32[8,4,4,3]{2,1,3,0:T(4,128)} %copy.23), calls=%async_computation | async-start | bytes 98304 | tf_op jit(solution)/shard_map/all_to_all | solution.py:65
  30.1 6.2 %all-to-all-done = s32[8,4,4,3]{2,1,3,0:T(4,128)S(1)} async-done(((s32[8,4,4,3]{2,1,3,0:T(4,128)}), s32[8,4,4,3]{2,1,3,0:T(4,128)S(1)}, u32[]{:S(2)}, u32[]{:S(2)}) %all-to-all-start) | async-done | bytes 1568 | tf_op jit(solution)/shard_map/all_to_all | solution.py:65
  36.3 3.2 %all-to-all-start.5 = ((s32[8,4,1]{0,2,1:T(1,128)}), s32[8,4,1]{0,2,1:T(1,128)S(1)}, u32[]{:S(2)}, u32[]{:S(2)}) async-start(s32[8,4,1]{0,2,1:T(1,128)} %copy.34), calls=%async_computation.5 | async-start | bytes 4096 | tf_op jit(solution)/shard_map/all_to_all | solution.py:71
  40.3 2.9 %all-to-all-done.5 = s32[8,4,1]{0,2,1:T(1,128)S(1)} async-done(((s32[8,4,1]{0,2,1:T(1,128)}), s32[8,4,1]{0,2,1:T(1,128)S(1)}, u32[]{:S(2)}, u32[]{:S(2)}) %all-to-all-start.5) | async-done | bytes 160 | tf_op jit(solution)/shard_map/all_to_all | solution.py:71
  43.2 3.3 %all-to-all-start.1 = ((s32[8,4,4,3]{0,2,3,1:T(4,128)}), s32[8,4,4,3]{0,2,3,1:T(4,128)S(1)}, u32[]{:S(2)}, u32[]{:S(2)}) async-start(s32[8,4,4,3]{0,2,3,1:T(4,128)} %copy.24), calls=%async_computation.1 | async-start | bytes 49152 | tf_op jit(solution)/shard_map/all_to_all | solution.py:64
  48.1 2.2 all-to-all-done.1
  50.3 3.3 %all-to-all-start.2 = ((bf16[8,4,4,96]{3,2,1,0:T(4,128)(2,1)}), bf16[8,4,4,96]{3,2,1,0:T(4,128)(2,1)S(1)}, u32[]{:S(2)}, u32[]{:S(2)}) async-start(bf16[8,4,4,96]{3,2,1,0:T(4,128)(2,1)} %bitcast.2), calls=%async_computation.2 | async-start | bytes 65536 | tf_op jit(solution)/shard_map/all_to_all | solution.py:53
  54.1 6.2 %all-to-all-done.2 = bf16[8,4,4,96]{3,2,1,0:T(4,128)(2,1)S(1)} async-done(((bf16[8,4,4,96]{3,2,1,0:T(4,128)(2,1)}), bf16[8,4,4,96]{3,2,1,0:T(4,128)(2,1)S(1)}, u32[]{:S(2)}, u32[]{:S(2)}) %all-to-all-start.2) | async-done | bytes 24608 | tf_op jit(solution)/shard_map/all_to_all | solution.py:53
  60.9 3.3 %all-to-all-start.3 = ((bf16[4,8,1,4,96]{4,3,1,2,0:T(4,128)(2,1)}), bf16[4,8,1,4,96]{4,3,1,2,0:T(4,128)(2,1)S(1)}, u32[]{:S(2)}, u32[]{:S(2)}) async-start(bf16[4,8,1,4,96]{4,3,1,2,0:T(4,128)(2,1)} %pad_maximum_fusion.1), calls=%async_computation.3 | async-start | bytes 65536 | tf_op jit(solution)/shard_map/all_to_all | solution.py:50
  64.2 4.3 %all-to-all-done.3 = bf16[4,8,1,4,96]{4,3,1,2,0:T(4,128)(2,1)S(1)} async-done(((bf16[4,8,1,4,96]{4,3,1,2,0:T(4,128)(2,1)}), bf16[4,8,1,4,96]{4,3,1,2,0:T(4,128)(2,1)S(1)}, u32[]{:S(2)}, u32[]{:S(2)}) %all-to-all-start.3) | async-done | bytes 24608 | tf_op jit(solution)/shard_map/all_to_all | solution.py:50
  68.5 27.9 %all-gather.3.cloned.1.call-done = bf16[32,1,75264]{2,1,0:T(2,128)(2,1)} async-done(((bf16[1,1,75264]{2,1,0:T(2,128)(2,1)}), bf16[32,1,75264]{2,1,0:T(2,128)(2,1)}) %all-gather.3.cloned.1.call-update) | async-done | bytes 4816912 | tf_op jit(solution)/shard_map/all_gather | solution.py:97
  96.4 87.6 %reduce = bf16[32,75264]{1,0:T(8,128)(2,1)} reduce(bf16[32,1,75264]{2,1,0:T(2,128)(2,1)} %all-gather.3.cloned.1.call-done, bf16[]{:T(256)} %constant.49), dimensions={1}, to_apply=%all-gather.reduce_sub_computation | reduce | bytes 9633794 | tf_op jit(solution)/shard_map/all_gather | solution.py:97
  184.1 9.6 %slice.107 = bf16[4704,512]{1,0:T(8,128)(2,1)} reshape(bf16[32,75264]{1,0:T(8,128)(2,1)} %reduce) | data formatting | bytes 9633792 | tf_op jit(solution)/shard_map/slice | solution.py:32
  193.7 10.3 %slice.103 = bf16[2352,1024]{1,0:T(8,128)(2,1)} reshape(bf16[32,75264]{1,0:T(8,128)(2,1)} %reduce) | data formatting | bytes 9633792 | tf_op jit(solution)/shard_map/slice | solution.py:32
  204.0 9.7 %reshape.98 = bf16[2408448]{0:T(1024)(128)(2,1)} reshape(bf16[32,75264]{1,0:T(8,128)(2,1)} %reduce) | data formatting | bytes 9633792 | tf_op jit(solution)/shard_map/reshape | solution.py:98
  228.7 5.1 %collective-permute-start.1 = (bf16[128,512]{1,0:T(8,128)(2,1)S(1)}, bf16[128,512]{1,0:T(8,128)(2,1)S(1)}, u32[]{:S(2)}, u32[]{:S(2)}) collective-permute-start(bf16[128,512]{1,0:T(8,128)(2,1)S(1)} %get-tuple-element.37), channel_id=1, source_target_pairs={{1,0},{2,1},{3,2},{4,3},{5,4},{6,5},{7,6},{8,7},{9,8},{10,9},{11,1... | collective-permute-start | bytes 393224 | tf_op jit(solution)/shard_map/ppermute | solution.py:22
  233.8 2.6 collective-permute-done
  236.5 2.2 gather_fusion.4
  238.7 2.0 gather_fusion
  240.8 2.0 gather_fusion.1
  244.8 2.0 gather_fusion.3
  246.8 2.0 gather_fusion.5
  248.9 3.5 %fusion.84 = (f32[320]{0:T(512)S(1)}, f32[320,512]{1,0:T(8,128)S(1)}) fusion(bf16[4704,512]{1,0:T(8,128)(2,1)} %slice.107, f32[320,1536]{1,0:T(8,128)} %get-tuple-element.54, f32[512]{0:T(512)S(1)} %bitcast.51, bf16[320,512]{1,0:T(8,128)(2,1)S(1)} %gather_fusion.5, bf16[320,512]{1,0:T(8,128)(2,1)S(1)} %gather_fusion.4, ...), kind=kOutput, calls=%fused_computation.136 | convolution fusion | flops 344882880 | bytes 4988992 | tf_op jit(solution)/shard_map/dot_general | solution.py:159
  (68 shorter events, 32.0 us)
Async XLA Ops:
  6.5 89.9 %all-gather.3.cloned.1.call-start = ((), (), s32[]{:S(2)}) async-start(), calls=%async_computation.6 | async-start | bytes 9934848 | tf_op jit(solution)/shard_map/all_gather | solution.py:97
  9.8 13.8 %all-to-all-start.4 = ((s32[8,1,4]{2,1,0:T(1,128)}), s32[8,1,4]{2,1,0:T(1,128)S(1)}, u32[]{:S(2)}, u32[]{:S(2)}) async-start(s32[8,1,4]{2,1,0:T(1,128)} %bitcast.10), calls=%async_computation.4 | async-start | bytes 8192 | tf_op jit(solution)/shard_map/all_to_all | solution.py:72
  23.5 12.8 %all-to-all-start = ((s32[8,4,4,3]{2,1,3,0:T(4,128)}), s32[8,4,4,3]{2,1,3,0:T(4,128)S(1)}, u32[]{:S(2)}, u32[]{:S(2)}) async-start(s32[8,4,4,3]{2,1,3,0:T(4,128)} %copy.23), calls=%async_computation | async-start | bytes 98304 | tf_op jit(solution)/shard_map/all_to_all | solution.py:65
  36.3 6.8 %all-to-all-start.5 = ((s32[8,4,1]{0,2,1:T(1,128)}), s32[8,4,1]{0,2,1:T(1,128)S(1)}, u32[]{:S(2)}, u32[]{:S(2)}) async-start(s32[8,4,1]{0,2,1:T(1,128)} %copy.34), calls=%async_computation.5 | async-start | bytes 4096 | tf_op jit(solution)/shard_map/all_to_all | solution.py:71
  43.2 7.1 %all-to-all-start.1 = ((s32[8,4,4,3]{0,2,3,1:T(4,128)}), s32[8,4,4,3]{0,2,3,1:T(4,128)S(1)}, u32[]{:S(2)}, u32[]{:S(2)}) async-start(s32[8,4,4,3]{0,2,3,1:T(4,128)} %copy.24), calls=%async_computation.1 | async-start | bytes 49152 | tf_op jit(solution)/shard_map/all_to_all | solution.py:64
  50.3 10.0 %all-to-all-start.2 = ((bf16[8,4,4,96]{3,2,1,0:T(4,128)(2,1)}), bf16[8,4,4,96]{3,2,1,0:T(4,128)(2,1)S(1)}, u32[]{:S(2)}, u32[]{:S(2)}) async-start(bf16[8,4,4,96]{3,2,1,0:T(4,128)(2,1)} %bitcast.2), calls=%async_computation.2 | async-start | bytes 65536 | tf_op jit(solution)/shard_map/all_to_all | solution.py:53
  60.9 7.6 %all-to-all-start.3 = ((bf16[4,8,1,4,96]{4,3,1,2,0:T(4,128)(2,1)}), bf16[4,8,1,4,96]{4,3,1,2,0:T(4,128)(2,1)S(1)}, u32[]{:S(2)}, u32[]{:S(2)}) async-start(bf16[4,8,1,4,96]{4,3,1,2,0:T(4,128)(2,1)} %pad_maximum_fusion.1), calls=%async_computation.3 | async-start | bytes 65536 | tf_op jit(solution)/shard_map/all_to_all | solution.py:50
  204.0 10.8 %copy-start.1 = (bf16[320,512]{1,0:T(8,128)(2,1)S(1)}, bf16[320,512]{1,0:T(8,128)(2,1)}, u32[]{:S(2)}) copy-start(bf16[320,512]{1,0:T(8,128)(2,1)} %param.14) | copy-start | bytes 983044
  221.6 0.8 copy-start
  221.6 1.6 slice-start
  228.4 8.0 %collective-permute-start = (bf16[128,512]{1,0:T(8,128)(2,1)S(1)}, bf16[128,512]{1,0:T(8,128)(2,1)S(1)}, u32[]{:S(2)}, u32[]{:S(2)}) collective-permute-start(bf16[128,512]{1,0:T(8,128)(2,1)S(1)} %get-tuple-element.36), channel_id=1, source_target_pairs={{0,1},{1,2},{2,3},{3,4},{4,5},{5,6},{6,7},{7,8},{8,9},{9,10},{10,1... | collective-permute-start | bytes 393224 | tf_op jit(solution)/shard_map/ppermute | solution.py:19
  228.7 7.8 %collective-permute-start.1 = (bf16[128,512]{1,0:T(8,128)(2,1)S(1)}, bf16[128,512]{1,0:T(8,128)(2,1)S(1)}, u32[]{:S(2)}, u32[]{:S(2)}) collective-permute-start(bf16[128,512]{1,0:T(8,128)(2,1)S(1)} %get-tuple-element.37), channel_id=1, source_target_pairs={{1,0},{2,1},{3,2},{4,3},{5,4},{6,5},{7,6},{8,7},{9,8},{10,9},{11,1... | collective-permute-start | bytes 393224 | tf_op jit(solution)/shard_map/ppermute | solution.py:22
Sparse Core Ops, SparseCore 0:
  10.2 86.2 all-gather.2
